TPU v7x, 512 devices: a whole 4x8x8 slice. The times are simulated.
512 devices in a mesh: dp: 16 (over z, core), mp: 32 (over y, x).
Axes of the slice: x: 4, y: 8, z: 8, core: 2. Of those that a mesh axis runs over, the one named last changes fastest.
Arguments:
- activations: bfloat16 [32768, 8192], P('dp', 'mp'), as said below
- output_grads: bfloat16 [32768, 28672], P('dp', 'mp'), as said below
- probe_matrix: bfloat16 [28672, 128], P('mp'), may hold values from -6 to 6
Outputs:
- basis: float32 [8192, 128], P('mp')
- projection: float32 [128, 28672], P(None, 'mp')
Inputs may be any that keep to these rules, and one draw needn't show every extreme that they name: `activations`: finite real values of order one. `output_grads`: finite real values of order one.
All inputs are finite; a program needn't handle non-finite values.
Results may differ from a plain program's by a relative error of at most 0.035.
Values may be sent and summed in bfloat16 or wider, within the bound.
No kernel may reach another device: no remote copies, remote signals or barrier semaphores. Data moves between devices by JAX's collectives and lax.ppermute only.
A program may use at most 64 MiB of HBM per device.

v0:
```python
import jax
import jax.numpy as jnp
from jax import lax
from jax.sharding import PartitionSpec as P

H = 8192


def contract_rows(left, right):
    return lax.dot_general(
        left, right, (((0,), (0,)), ((), ())), preferred_element_type=jnp.float32
    )


def token_total(partial_value):
    return lax.psum(partial_value.astype(jnp.bfloat16), "mp")


def gram_of(matrix):
    return lax.dot_general(
        matrix,
        matrix,
        (((0,), (0,)), ((), ())),
        precision=lax.Precision.HIGHEST,
        preferred_element_type=jnp.float32,
    )


def solve_rows(factor, matrix):
    return lax.linalg.triangular_solve(
        factor, matrix, left_side=False, lower=True, transpose_a=True
    )


def orthonormalize(partial_value):
    summed = lax.psum(partial_value, "dp")
    gram_matrix = lax.psum(gram_of(summed), "mp")
    factor = jnp.linalg.cholesky(gram_matrix)
    return solve_rows(factor, summed)


def on_device(activations, output_grads, probe_matrix):
    probe_rows = token_total(
        jnp.dot(output_grads, probe_matrix, preferred_element_type=jnp.float32)
    )
    first_basis = orthonormalize(contract_rows(activations, probe_rows))
    token_rows = token_total(
        jnp.dot(activations, first_basis.astype(jnp.bfloat16), preferred_element_type=jnp.float32)
    )
    second_basis = orthonormalize(contract_rows(output_grads, token_rows))
    unit_rows = token_total(
        jnp.dot(output_grads, second_basis.astype(jnp.bfloat16), preferred_element_type=jnp.float32)
    )
    third_basis = orthonormalize(contract_rows(activations, unit_rows))
    last_rows = token_total(
        jnp.dot(activations, third_basis.astype(jnp.bfloat16), preferred_element_type=jnp.float32)
    )
    projected = contract_rows(last_rows, output_grads)
    projection = lax.psum(projected, "dp")
    basis = third_basis * jnp.sqrt(jnp.float32(H))
    return (basis, projection)


def solution(mesh):
    in_specs = (P("dp", "mp"), P("dp", "mp"), P("mp", None))
    out_specs = (P("mp", None), P(None, "mp"))
    return jax.shard_map(
        on_device, mesh=mesh, in_specs=in_specs, out_specs=out_specs, check_vma=False
    )
```

profile of v0, /device:TPU:1, one launch (start us, length us, event | category | flops | bytes accessed | tf_op | source)
XLA Modules:
  0.0 1659.9 jit_solution(11712549844243807659)
XLA Ops:
  7.2 0.0 all-reduce.12.cloned.1.call-start
  7.2 4.1 convolution_convert_fusion.1
  11.3 0.0 all-reduce.12.cloned.1.call-update
  11.3 0.0 all-reduce.14.cloned.1.call-start
  11.4 159.3 %all-reduce.12.cloned.1.call-done = bf16[2048,128]{1,0:T(8,128)(2,1)} async-done(((bf16[2048,128]{1,0:T(8,128)(2,1)}), bf16[2048,128]{1,0:T(8,128)(2,1)}) %all-reduce.12.cloned.1.call-update) | async-done | bytes 524304 | tf_op jit(solution)/shard_map/psum | solution.py:16
  170.7 2.0 convolution_bitcast_fusion.4
  172.7 0.0 all-reduce.14.cloned.1.call-update
  172.8 0.0 all-reduce.16.cloned.1.call-start
  172.8 116.4 %all-reduce.14.cloned.1.call-done = f32[256,128]{0,1:T(8,128)} async-done(((f32[256,128]{0,1:T(8,128)}), f32[256,128]{0,1:T(8,128)}) %all-reduce.14.cloned.1.call-update) | async-done | bytes 131088 | tf_op jit(solution)/shard_map/psum | solution.py:36
  289.2 1.9 fusion.18
  291.1 0.0 all-reduce.16.cloned.1.call-update
  291.1 0.0 all-reduce.18.cloned.1.call-start
  291.2 148.2 %all-reduce.16.cloned.1.call-done = f32[128,128]{0,1:T(8,128)} async-done(((f32[128,128]{0,1:T(8,128)}), f32[128,128]{0,1:T(8,128)}) %all-reduce.16.cloned.1.call-update) | async-done | bytes 65552 | tf_op jit(solution)/shard_map/psum | solution.py:37
  439.4 0.9 copy.6
  440.3 0.9 fusion.12
  441.2 11.7 cholesky.59
  452.9 0.6 compare_reduce_fusion.2
  453.5 0.7 fusion.4
  454.2 9.8 custom-call.10
  464.0 1.2 fusion.3
  465.2 1.3 fusion.1
  466.5 0.0 all-reduce.18.cloned.1.call-update
  466.6 0.0 all-reduce.20.cloned.1.call-start
  466.6 156.5 %all-reduce.18.cloned.1.call-done = bf16[2048,128]{0,1:T(8,128)(2,1)} async-done(((bf16[2048,128]{0,1:T(8,128)(2,1)}), bf16[2048,128]{0,1:T(8,128)(2,1)}) %all-reduce.18.cloned.1.call-update) | async-done | bytes 524304 | tf_op jit(solution)/shard_map/psum | solution.py:16
  623.1 3.7 convolution_bitcast_fusion
  626.8 0.0 all-reduce.22.cloned.1.call-start
  626.8 116.4 %all-reduce.20.cloned.1.call-done = f32[896,128]{0,1:T(8,128)} async-done(((f32[896,128]{0,1:T(8,128)}), f32[896,128]{0,1:T(8,128)}) %all-reduce.20.cloned.1.call-update) | async-done | bytes 458768 | tf_op jit(solution)/shard_map/psum | solution.py:36
  743.2 2.4 fusion.19
  745.6 0.0 all-reduce.22.cloned.1.call-update
  745.6 0.2 all-reduce.24.cloned.1.call-start
  745.8 145.9 %all-reduce.22.cloned.1.call-done = f32[128,128]{0,1:T(8,128)} async-done(((f32[128,128]{0,1:T(8,128)}), f32[128,128]{0,1:T(8,128)}) %all-reduce.22.cloned.1.call-update) | async-done | bytes 65552 | tf_op jit(solution)/shard_map/psum | solution.py:37
  891.7 0.9 copy.8
  892.7 0.9 fusion.10
  893.5 11.7 cholesky.70
  905.3 0.6 compare_reduce_fusion.1
  905.9 0.7 fusion.5
  906.6 9.8 custom-call.8
  916.4 1.9 convolution_convert_fusion.4
  918.3 4.2 fusion
  922.5 0.0 all-reduce.24.cloned.1.call-update
  922.5 0.0 all-reduce.26.cloned.1.call-start
  922.6 156.4 %all-reduce.24.cloned.1.call-done = bf16[2048,128]{0,1:T(8,128)(2,1)} async-done(((bf16[2048,128]{0,1:T(8,128)(2,1)}), bf16[2048,128]{0,1:T(8,128)(2,1)}) %all-reduce.24.cloned.1.call-update) | async-done | bytes 524304 | tf_op jit(solution)/shard_map/psum | solution.py:16
  1079.0 2.0 convolution_bitcast_fusion.3
  1081.0 0.0 all-reduce.26.cloned.1.call-update
  1081.0 0.0 all-reduce.28.cloned.1.call-start
  1081.1 116.5 %all-reduce.26.cloned.1.call-done = f32[256,128]{0,1:T(8,128)} async-done(((f32[256,128]{0,1:T(8,128)}), f32[256,128]{0,1:T(8,128)}) %all-reduce.26.cloned.1.call-update) | async-done | bytes 131088 | tf_op jit(solution)/shard_map/psum | solution.py:36
  1197.5 1.9 fusion.20
  1199.4 0.0 all-reduce.28.cloned.1.call-update
  1199.4 0.3 all-reduce.30.cloned.1.call-start
  1199.7 147.9 %all-reduce.28.cloned.1.call-done = f32[128,128]{0,1:T(8,128)} async-done(((f32[128,128]{0,1:T(8,128)}), f32[128,128]{0,1:T(8,128)}) %all-reduce.28.cloned.1.call-update) | async-done | bytes 65552 | tf_op jit(solution)/shard_map/psum | solution.py:37
  1347.7 0.9 copy.10
  1348.6 0.9 fusion.8
  1349.4 11.7 cholesky.81
  1361.2 0.6 compare_reduce_fusion
  1361.8 0.7 fusion.6
  1362.5 9.8 custom-call.11
  1372.3 1.2 broadcast_multiply_fusion
  1373.5 1.3 fusion.2
  1374.9 0.0 all-reduce.32.cloned.1.call-start
  1374.9 156.5 %all-reduce.30.cloned.1.call-done = bf16[2048,128]{0,1:T(8,128)(2,1)} async-done(((bf16[2048,128]{0,1:T(8,128)(2,1)}), bf16[2048,128]{0,1:T(8,128)(2,1)}) %all-reduce.30.cloned.1.call-update) | async-done | bytes 524304 | tf_op jit(solution)/shard_map/psum | solution.py:16
  1531.4 3.7 fusion.21
  1535.1 0.8 copy.11
  1535.9 115.7 %all-reduce.32.cloned.1.call-done = f32[128,896]{1,0:T(8,128)} async-done(((f32[128,896]{1,0:T(8,128)}), f32[128,896]{1,0:T(8,128)}) %all-reduce.32.cloned.1.call-update) | async-done | bytes 458768 | tf_op jit(solution)/shard_map/psum | solution.py:59
  1651.5 1.8 copy.26
  (8 shorter events, 0.2 us)
Async XLA Ops:
  7.2 163.5 %copy-start = (bf16[2048,256]{1,0:T(8,128)(2,1)S(1)}, bf16[2048,256]{1,0:T(8,128)(2,1)}, u32[]{:S(2)}) copy-start(bf16[2048,256]{1,0:T(8,128)(2,1)} %param.6) | copy-start | bytes 3145732
  7.2 163.5 %all-reduce.12.cloned.1.call-start = ((), (), s32[]{:S(2)}) async-start(), calls=%async_computation | async-start | bytes 1048576 | tf_op jit(solution)/shard_map/psum | solution.py:16
  11.3 277.9 %all-reduce.14.cloned.1.call-start = ((), (), s32[]{:S(2)}) async-start(), calls=%async_computation.1 | async-start | bytes 262144 | tf_op jit(solution)/shard_map/psum | solution.py:36
  172.8 266.6 %all-reduce.16.cloned.1.call-start = ((), (), s32[]{:S(2)}) async-start(), calls=%async_computation.2 | async-start | bytes 131072 | tf_op jit(solution)/shard_map/psum | solution.py:37
  291.1 331.9 %all-reduce.18.cloned.1.call-start = ((), (), s32[]{:S(2)}) async-start(), calls=%async_computation.3 | async-start | bytes 1048576 | tf_op jit(solution)/shard_map/psum | solution.py:16
  466.6 276.6 %all-reduce.20.cloned.1.call-start = ((), (), s32[]{:S(2)}) async-start(), calls=%async_computation.4 | async-start | bytes 917504 | tf_op jit(solution)/shard_map/psum | solution.py:36
  626.8 264.9 %all-reduce.22.cloned.1.call-start = ((), (), s32[]{:S(2)}) async-start(), calls=%async_computation.5 | async-start | bytes 131072 | tf_op jit(solution)/shard_map/psum | solution.py:37
  745.6 333.4 %all-reduce.24.cloned.1.call-start = ((), (), s32[]{:S(2)}) async-start(), calls=%async_computation.6 | async-start | bytes 1048576 | tf_op jit(solution)/shard_map/psum | solution.py:16
  922.5 275.0 %all-reduce.26.cloned.1.call-start = ((), (), s32[]{:S(2)}) async-start(), calls=%async_computation.7 | async-start | bytes 262144 | tf_op jit(solution)/shard_map/psum | solution.py:36
  1081.0 266.7 %all-reduce.28.cloned.1.call-start = ((), (), s32[]{:S(2)}) async-start(), calls=%async_computation.8 | async-start | bytes 131072 | tf_op jit(solution)/shard_map/psum | solution.py:37
  1199.4 331.9 %all-reduce.30.cloned.1.call-start = ((), (), s32[]{:S(2)}) async-start(), calls=%async_computation.9 | async-start | bytes 1048576 | tf_op jit(solution)/shard_map/psum | solution.py:16
  1374.9 276.7 %all-reduce.32.cloned.1.call-start = ((), (), s32[]{:S(2)}) async-start(), calls=%async_computation.10 | async-start | bytes 917504 | tf_op jit(solution)/shard_map/psum | solution.py:59
Sparse Core Ops, SparseCore 0:
  11.4 159.2 all-reduce.11
  173.7 115.5 all-reduce.13
  293.3 146.0 all-reduce.15
  466.7 156.3 all-reduce.17
  626.9 116.2 all-reduce.19
  747.1 144.5 all-reduce.21
  922.6 156.2 all-reduce.23
  1082.0 115.5 all-reduce.25
  1201.6 146.0 all-reduce.27
  1375.0 156.3 all-reduce.29
  1535.2 116.2 all-reduce.31
where the time goes:
time: 1660 us
  waiting for transfers between devices  1540 us (93%)
  other arithmetic  71.1 us (4%)
  matrix products  32.8 us (2%)
    psum x4, waiting for transfers between devices, token_total(): return lax.psum(partial_value.astype(jnp.bfloat16), 'mp')  629 us
    psum x3, waiting for transfers between devices, orthonormalize(): gram_matrix = lax.psum(gram_of(summed), 'mp')  442 us
    psum x3, waiting for transfers between devices, orthonormalize(): summed = lax.psum(partial_value, 'dp')  349 us
    psum x1, waiting for transfers between devices, on_device(): projection = lax.psum(projected, 'dp')  116 us
    another operation x9, other arithmetic, orthonormalize(): factor = jnp.linalg.cholesky(gram_matrix)  37.2 us
  transfers between devices with their start and end apart: 11, of which 11 were waited for; matrix products, arithmetic and copies ran while one was open for 0% of the time, Pallas kernels for 0%

commit v1 on v0

--- a/solution.py
+++ b/solution.py
@@ -34,7 +34,9 @@
 
 def orthonormalize(partial_value):
     summed = lax.psum(partial_value, "dp")
-    gram_matrix = lax.psum(gram_of(summed), "mp")
+    part = gram_of(summed)
+    terms = lax.all_gather(part, "mp", axis=0, tiled=False)
+    gram_matrix = terms.sum(axis=0)
     factor = jnp.linalg.cholesky(gram_matrix)
     return solve_rows(factor, summed)
 

time: 1660 us -> 1450 us (0.87)
  waiting for transfers between devices: 1540 us -> 1330 us
    psum x3 -> x0, waiting for transfers between devices: 442 us -> none  [orthonormalize(): gram_matrix = lax.psum(gram_of(summed), 'mp')]
    all_gather x0 -> x3, waiting for transfers between devices: none -> 241 us  [orthonormalize(): terms = lax.all_gather(part, 'mp', axis=0, tiled=False)]
where the time goes in v1:
time: 1450 us
  waiting for transfers between devices  1330 us (92%)
  other arithmetic  73.7 us (5%)
  matrix products  31.8 us (2%)
    psum x4, waiting for transfers between devices, token_total(): return lax.psum(partial_value.astype(jnp.bfloat16), 'mp')  624 us
    psum x3, waiting for transfers between devices, orthonormalize(): summed = lax.psum(partial_value, 'dp')  349 us
    all_gather x3, waiting for transfers between devices, orthonormalize(): terms = lax.all_gather(part, 'mp', axis=0, tiled=False)  241 us
    psum x1, waiting for transfers between devices, on_device(): projection = lax.psum(projected, 'dp')  115 us
    another operation x9, other arithmetic, orthonormalize(): factor = jnp.linalg.cholesky(gram_matrix)  37.2 us
    another operation x6, other arithmetic, solve_rows(): lax.linalg.triangular_solve(factor, matrix, left_side=False, lower=True,...  31.4 us
  transfers between devices with their start and end apart: 11, of which 11 were waited for; matrix products, arithmetic and copies ran while one was open for 0% of the time, Pallas kernels for 0%

profile of v1, /device:TPU:1, one launch (start us, length us, event | category | flops | bytes accessed | tf_op | source)
XLA Modules:
  0.0 1453.1 jit_solution(6361867439550280717)
XLA Ops:
  7.2 0.0 all-reduce.9.cloned.1.call-start
  7.2 4.1 convolution_convert_fusion.1
  11.3 0.0 all-reduce.9.cloned.1.call-update
  11.3 0.0 all-reduce.11.cloned.1.call-start
  11.4 159.3 %all-reduce.9.cloned.1.call-done = bf16[2048,128]{1,0:T(8,128)(2,1)} async-done(((bf16[2048,128]{1,0:T(8,128)(2,1)}), bf16[2048,128]{1,0:T(8,128)(2,1)}) %all-reduce.9.cloned.1.call-update) | async-done | bytes 524304 | tf_op jit(solution)/shard_map/psum | solution.py:16
  170.7 2.0 convolution_bitcast_fusion.4
  172.7 0.0 all-reduce.11.cloned.1.call-update
  172.8 0.0 all-gather.7.cloned.1.call-start
  172.8 116.4 %all-reduce.11.cloned.1.call-done = f32[256,128]{0,1:T(8,128)} async-done(((f32[256,128]{0,1:T(8,128)}), f32[256,128]{0,1:T(8,128)}) %all-reduce.11.cloned.1.call-update) | async-done | bytes 131088 | tf_op jit(solution)/shard_map/psum | solution.py:36
  289.2 1.9 fusion.18
  291.1 0.0 all-reduce.13.cloned.1.call-start
  291.2 81.0 %all-gather.7.cloned.1.call-done = f32[4096,128]{1,0:T(8,128)} async-done(((f32[128,128]{1,0:T(8,128)}), f32[4096,128]{1,0:T(8,128)}) %all-gather.7.cloned.1.call-update) | async-done | bytes 2097168 | tf_op jit(solution)/shard_map/all_gather | solution.py:38
  372.2 1.7 reduce_sum.27
  373.9 0.1 copy.9
  374.1 11.7 cholesky.59
  385.8 0.6 compare_reduce_fusion.2
  386.5 0.7 fusion.4
  387.1 9.8 custom-call.10
  396.9 1.2 fusion.3
  398.1 1.3 fusion.1
  399.4 0.0 all-reduce.13.cloned.1.call-update
  399.5 0.0 all-reduce.15.cloned.1.call-start
  399.5 155.1 %all-reduce.13.cloned.1.call-done = bf16[2048,128]{0,1:T(8,128)(2,1)} async-done(((bf16[2048,128]{0,1:T(8,128)(2,1)}), bf16[2048,128]{0,1:T(8,128)(2,1)}) %all-reduce.13.cloned.1.call-update) | async-done | bytes 524304 | tf_op jit(solution)/shard_map/psum | solution.py:16
  554.6 3.7 convolution_bitcast_fusion
  558.3 0.0 all-reduce.15.cloned.1.call-update
  558.3 0.0 all-gather.9.cloned.1.call-start
  558.4 116.2 %all-reduce.15.cloned.1.call-done = f32[896,128]{0,1:T(8,128)} async-done(((f32[896,128]{0,1:T(8,128)}), f32[896,128]{0,1:T(8,128)}) %all-reduce.15.cloned.1.call-update) | async-done | bytes 458768 | tf_op jit(solution)/shard_map/psum | solution.py:36
  674.6 2.5 fusion.19
  677.0 0.0 all-gather.9.cloned.1.call-update
  677.1 0.2 all-reduce.17.cloned.1.call-start
  677.3 78.7 %all-gather.9.cloned.1.call-done = f32[4096,128]{1,0:T(8,128)} async-done(((f32[128,128]{1,0:T(8,128)}), f32[4096,128]{1,0:T(8,128)}) %all-gather.9.cloned.1.call-update) | async-done | bytes 2097168 | tf_op jit(solution)/shard_map/all_gather | solution.py:38
  756.0 1.7 reduce_sum.28
  757.7 0.1 copy.10
  757.8 11.7 cholesky.70
  769.5 0.6 compare_reduce_fusion.1
  770.2 0.7 fusion.5
  770.8 9.8 custom-call.8
  780.6 0.9 convolution_convert_fusion.4
  781.5 4.2 fusion
  785.7 0.0 all-reduce.17.cloned.1.call-update
  785.8 0.0 all-reduce.19.cloned.1.call-start
  785.8 155.1 %all-reduce.17.cloned.1.call-done = bf16[2048,128]{0,1:T(8,128)(2,1)} async-done(((bf16[2048,128]{0,1:T(8,128)(2,1)}), bf16[2048,128]{0,1:T(8,128)(2,1)}) %all-reduce.17.cloned.1.call-update) | async-done | bytes 524304 | tf_op jit(solution)/shard_map/psum | solution.py:16
  940.9 2.0 convolution_bitcast_fusion.3
  942.9 0.0 all-reduce.19.cloned.1.call-update
  942.9 0.0 all-gather.11.cloned.1.call-start
  943.0 116.5 %all-reduce.19.cloned.1.call-done = f32[256,128]{0,1:T(8,128)} async-done(((f32[256,128]{0,1:T(8,128)}), f32[256,128]{0,1:T(8,128)}) %all-reduce.19.cloned.1.call-update) | async-done | bytes 131088 | tf_op jit(solution)/shard_map/psum | solution.py:36
  1059.4 1.9 fusion.20
  1061.3 0.0 all-gather.11.cloned.1.call-update
  1061.4 0.3 all-reduce.21.cloned.1.call-start
  1061.6 80.8 %all-gather.11.cloned.1.call-done = f32[4096,128]{1,0:T(8,128)} async-done(((f32[128,128]{1,0:T(8,128)}), f32[4096,128]{1,0:T(8,128)}) %all-gather.11.cloned.1.call-update) | async-done | bytes 2097168 | tf_op jit(solution)/shard_map/all_gather | solution.py:38
  1142.5 1.7 reduce_sum.29
  1144.2 0.1 copy.11
  1144.3 11.7 cholesky.81
  1156.0 0.6 compare_reduce_fusion
  1156.7 0.7 fusion.6
  1157.3 9.8 custom-call.11
  1167.1 1.2 broadcast_multiply_fusion
  1168.4 1.3 fusion.2
  1169.7 0.0 all-reduce.23.cloned.1.call-start
  1169.7 155.0 %all-reduce.21.cloned.1.call-done = bf16[2048,128]{0,1:T(8,128)(2,1)} async-done(((bf16[2048,128]{0,1:T(8,128)(2,1)}), bf16[2048,128]{0,1:T(8,128)(2,1)}) %all-reduce.21.cloned.1.call-update) | async-done | bytes 524304 | tf_op jit(solution)/shard_map/psum | solution.py:16
  1324.7 3.7 fusion.21
  1328.5 0.8 copy.12
  1329.2 115.5 %all-reduce.23.cloned.1.call-done = f32[128,896]{1,0:T(8,128)} async-done(((f32[128,896]{1,0:T(8,128)}), f32[128,896]{1,0:T(8,128)}) %all-reduce.23.cloned.1.call-update) | async-done | bytes 458768 | tf_op jit(solution)/shard_map/psum | solution.py:61
  1444.7 1.8 copy.21
  (13 shorter events, 0.2 us)
Async XLA Ops:
  7.2 163.5 %copy-start = (bf16[2048,256]{1,0:T(8,128)(2,1)S(1)}, bf16[2048,256]{1,0:T(8,128)(2,1)}, u32[]{:S(2)}) copy-start(bf16[2048,256]{1,0:T(8,128)(2,1)} %param.6) | copy-start | bytes 3145732
  7.2 163.5 %all-reduce.9.cloned.1.call-start = ((), (), s32[]{:S(2)}) async-start(), calls=%async_computation | async-start | bytes 1048576 | tf_op jit(solution)/shard_map/psum | solution.py:16
  11.3 277.9 %all-reduce.11.cloned.1.call-start = ((), (), s32[]{:S(2)}) async-start(), calls=%async_computation.1 | async-start | bytes 262144 | tf_op jit(solution)/shard_map/psum | solution.py:36
  172.8 199.5 %all-gather.7.cloned.1.call-start = ((), (), s32[]{:S(2)}) async-start(), calls=%async_computation.8 | async-start | bytes 2162688 | tf_op jit(solution)/shard_map/all_gather | solution.py:38
  291.1 263.4 %all-reduce.13.cloned.1.call-start = ((), (), s32[]{:S(2)}) async-start(), calls=%async_computation.2 | async-start | bytes 1048576 | tf_op jit(solution)/shard_map/psum | solution.py:16
  399.5 275.1 %all-reduce.15.cloned.1.call-start = ((), (), s32[]{:S(2)}) async-start(), calls=%async_computation.3 | async-start | bytes 917504 | tf_op jit(solution)/shard_map/psum | solution.py:36
  558.3 197.6 %all-gather.9.cloned.1.call-start = ((), (), s32[]{:S(2)}) async-start(), calls=%async_computation.9 | async-start | bytes 2162688 | tf_op jit(solution)/shard_map/all_gather | solution.py:38
  674.6 106.1 %copy-start.1 = (f32[896,128]{0,1:T(8,128)S(1)}, f32[896,128]{0,1:T(8,128)}, u32[]{:S(2)}) copy-start(f32[896,128]{0,1:T(8,128)} %all-reduce.15.cloned.1.call-done) | copy-start | bytes 1376260
  677.1 263.8 %all-reduce.17.cloned.1.call-start = ((), (), s32[]{:S(2)}) async-start(), calls=%async_computation.4 | async-start | bytes 1048576 | tf_op jit(solution)/shard_map/psum | solution.py:16
  785.8 273.7 %all-reduce.19.cloned.1.call-start = ((), (), s32[]{:S(2)}) async-start(), calls=%async_computation.5 | async-start | bytes 262144 | tf_op jit(solution)/shard_map/psum | solution.py:36
  942.9 199.5 %all-gather.11.cloned.1.call-start = ((), (), s32[]{:S(2)}) async-start(), calls=%async_computation.10 | async-start | bytes 2162688 | tf_op jit(solution)/shard_map/all_gather | solution.py:38
  1061.4 263.4 %all-reduce.21.cloned.1.call-start = ((), (), s32[]{:S(2)}) async-start(), calls=%async_computation.6 | async-start | bytes 1048576 | tf_op jit(solution)/shard_map/psum | solution.py:16
  1169.7 275.0 %all-reduce.23.cloned.1.call-start = ((), (), s32[]{:S(2)}) async-start(), calls=%async_computation.7 | async-start | bytes 917504 | tf_op jit(solution)/shard_map/psum | solution.py:61
Sparse Core Ops, SparseCore 0:
  11.4 159.2 all-reduce.8
  173.7 115.5 all-reduce.10
  293.0 79.2 all-gather.6
  399.6 154.9 all-reduce.12
  558.4 116.0 all-reduce.14
  678.2 77.7 all-gather.8
  785.9 154.9 all-reduce.16
  943.9 115.5 all-reduce.18
  1063.2 79.2 all-gather.10
  1169.8 154.9 all-reduce.20
  1328.6 116.0 all-reduce.22
